TPU v7x, 256 devices: a whole 4x4x8 slice. The times are simulated.
256 devices in a mesh: req: 8 (over z), row: 8 (over x, core), col: 4 (over y).
Axes of the slice: x: 4, y: 4, z: 8, core: 2. Of those that a mesh axis runs over, the one named last changes fastest.
Arguments:
- hidden: bfloat16 [4096, 2048], P('req'), as said below
- attention_gain: float32 [2048], replicated, may hold values from 0.5 to 2
- query_weight: bfloat16 [2048, 2048], P('row', 'col'), may hold values from -0.125 to 0.125
- key_value_weight: bfloat16 [2048, 4, 128], P('row', 'col'), may hold values from -0.125 to 0.125
- output_weight: bfloat16 [2048, 2048], P('col', 'row'), may hold values from -0.75 to 0.75
- final_gain: float32 [2048], replicated, may hold values from 0.5 to 2
- head_weight: bfloat16 [2048, 32064], P(None, ('row', 'col')), as said below
- key_value_cache: bfloat16 [64, 2048, 4, 128], P(('req', 'row'), None, 'col'), as said below
- parents: int32 [64, 64], P('req'), may hold values from 0 to 62, as said below
- counts: int32 [64], P('req'), may hold values from 32 to 64, as said below
- lengths: int32 [64], P('req'), may hold values from 1 to 32768
- tokens: int32 [64, 64], P('req'), may hold values from 0 to 32063
- accepted_path: int32 [64, 8], P('req'), may hold values from 0 to 28, as said below
- accept_count: int32 [64], P('req'), may hold values from 1 to 8
Outputs:
- node_logprob: float32 [64, 64], P('req')
- next_logprob: float32 [64, 32064], P('req', ('row', 'col'))
- accepted_cache: bfloat16 [64, 8, 4, 128], P(('req', 'row'), None, 'col')
Inputs may be any that keep to these rules, and one draw needn't show every extreme that they name: `hidden`: real values. `head_weight`: real values. `key_value_cache`: real values; slots that the lengths leave empty hold values that must not be used. `parents`: for node i >= 1 the parent is below i and at least i - 4; the entry of node 0 is 0. Nodes 0 to counts[b] - 1 of request b are live, and every ancestor of a live node is live. accepted_path[b, 0] = 0, each entry below accept_count[b] is a live child of the one before, and the entries from accept_count[b] on are 0.
All inputs are finite; a program needn't handle non-finite values.
Results may differ from a plain program's by a relative error of at most 0.0093.
Values may be sent and summed in bfloat16 or wider, within the bound.
A program may use at most 64 MiB of HBM per device.

v0:
```python
import math

import jax
import jax.numpy as jnp
from jax import lax
from jax.sharding import PartitionSpec as P

D = 2048
NODES = 64


epsilon = 1e-05


def combined_all(value, axis, combine):
    everything = jax.tree.map(lambda part: lax.all_gather(part, axis), value)
    initial = jax.tree.map(lambda part: part[0], everything)

    def turn(k, so_far):
        return combine(so_far, jax.tree.map(lambda part: part[k], everything))

    return lax.fori_loop(1, lax.axis_size(axis), turn, initial)


def ancestry(parents):
    node_count = parents.shape[1]
    node_ids = jnp.arange(node_count, dtype=jnp.int32)
    linked = (parents[:, :, None] == node_ids[None, None, :]) & (node_ids[None, :, None] > 0)
    reached = jnp.eye(node_count, dtype=jnp.float32)[None] + linked.astype(jnp.float32)
    for sweep in range(node_count.bit_length()):
        reached = jnp.minimum(
            jnp.einsum("bij,bjk->bik", reached, reached, precision=lax.Precision.HIGHEST), 1.0
        )
    return (reached, jnp.sum(reached, axis=2) - 1.0)


def rotate(values, positions):
    half_size = values.shape[-1] // 2
    frequency = 10000.0 ** (-jnp.arange(half_size, dtype=jnp.float32) / half_size)
    angles = positions[..., None, None] * frequency
    cosine = jnp.cos(angles)
    sine_part = jnp.sin(angles)
    front_half = values[..., :half_size]
    back_half = values[..., half_size:]
    return jnp.concatenate(
        [front_half * cosine - back_half * sine_part, back_half * cosine + front_half * sine_part],
        axis=-1,
    )


def attend(queries, new_keys, new_values, cache_rows, reached, depths, length):
    node_count, head_count, head_size = queries.shape
    group_count = new_keys.shape[1]
    window_size = cache_rows.shape[0]
    grouped = queries.reshape(node_count, group_count, head_count // group_count, head_size)
    all_keys = jnp.concatenate([cache_rows[:, :, :head_size], new_keys], axis=0)
    all_values = jnp.concatenate([cache_rows[:, :, head_size:], new_values], axis=0)
    scores = jnp.einsum("ngqd,kgd->gqnk", grouped, all_keys, preferred_element_type=jnp.float32) * (
        1.0 / math.sqrt(head_size)
    )
    slot_ids = jnp.arange(window_size, dtype=jnp.float32)
    cache_open = (slot_ids[None, :] > depths[:, None]) & (
        slot_ids[None, :] >= (window_size - length).astype(jnp.float32)
    )
    allowed = jnp.concatenate([cache_open, reached > 0.5], axis=1)
    scores = jnp.where(allowed[None, None], scores, -jnp.inf)
    row_max = jnp.max(scores, axis=3, keepdims=True)
    weights = jnp.exp(scores - row_max)
    weights_bf = (weights / jnp.sum(weights, axis=3, keepdims=True)).astype(jnp.bfloat16)
    attended = jnp.einsum(
        "gqnk,kgd->ngqd", weights_bf, all_values, preferred_element_type=jnp.float32
    )
    return attended.reshape(node_count, head_count * head_size).astype(jnp.bfloat16)


def attend_packed(packed):
    return attend(*packed)


def combine_parts(first_part, second_part):
    larger = jnp.maximum(first_part[0], second_part[0])
    summed = first_part[1] * jnp.exp(first_part[0] - larger) + second_part[1] * jnp.exp(
        second_part[0] - larger
    )
    return (larger, summed, first_part[2] + second_part[2])


def shards(
    hidden,
    attention_gain,
    query_weight,
    key_value_weight,
    output_weight,
    final_gain,
    head_weight,
    key_value_cache,
    parents,
    counts,
    lengths,
    tokens,
    accepted_path,
    accept_count,
):
    group_requests = parents.shape[0]
    local_requests = key_value_cache.shape[0]
    row_slot = lax.axis_index("row")
    row_width = query_weight.shape[0]
    query_width = query_weight.shape[1]
    group_count = key_value_weight.shape[1]
    head_size = key_value_weight.shape[2] // 2
    widened = hidden.astype(jnp.float32)
    inverse_norm = lax.rsqrt(jnp.mean(widened * widened, axis=1, keepdims=True) + epsilon)
    wide_part = lax.dynamic_slice_in_dim(widened, row_slot * row_width, row_width, 1)
    pair_weight = key_value_weight.reshape(row_width, group_count * 2 * head_size)
    gain_part = lax.dynamic_slice_in_dim(attention_gain, row_slot * row_width, row_width, 0)
    normed = (wide_part * inverse_norm * gain_part).astype(jnp.bfloat16)
    joint_weight = jnp.concatenate([query_weight, pair_weight], axis=1)
    own_terms = lax.psum_scatter(
        jnp.dot(normed, joint_weight, preferred_element_type=jnp.float32),
        "row",
        scatter_dimension=0,
        tiled=True,
    )
    own_parents = lax.dynamic_slice_in_dim(parents, row_slot * local_requests, local_requests, 0)
    own_lengths = lax.dynamic_slice_in_dim(lengths, row_slot * local_requests, local_requests, 0)
    reached, depths = ancestry(own_parents)
    positions = own_lengths[:, None].astype(jnp.float32) + depths
    raw_queries = own_terms[:, :query_width].reshape(
        local_requests, NODES, query_width // head_size, head_size
    )
    queries = rotate(raw_queries, positions).astype(jnp.bfloat16)
    raw_pairs = own_terms[:, query_width:].reshape(
        local_requests, NODES, group_count, 2 * head_size
    )
    new_keys = rotate(raw_pairs[..., :head_size], positions).astype(jnp.bfloat16)
    new_values = raw_pairs[..., head_size:].astype(jnp.bfloat16)
    attended = lax.map(
        attend_packed,
        (queries, new_keys, new_values, key_value_cache, reached, depths, own_lengths),
    )
    attended = attended.reshape(local_requests * NODES, query_width)
    head_terms = jnp.dot(
        lax.all_gather(attended, "row", axis=0, tiled=True),
        output_weight,
        preferred_element_type=jnp.float32,
    )
    vocab_width = head_weight.shape[1]
    col_share = lax.psum_scatter(head_terms, "col", scatter_dimension=1, tiled=True)
    share_width = col_share.shape[1]
    share_start = row_slot * row_width + lax.axis_index("col") * share_width
    residual = lax.dynamic_slice_in_dim(widened, share_start, share_width, 1) + col_share
    squares = lax.psum(jnp.sum(residual * residual, axis=1), ("row", "col"))
    final_part = lax.dynamic_slice_in_dim(final_gain, share_start, share_width, 0)
    normed_out = (residual * lax.rsqrt(squares / D + epsilon)[:, None] * final_part).astype(
        jnp.bfloat16
    )
    logits = jnp.dot(
        lax.all_gather(normed_out, ("row", "col"), axis=1, tiled=True),
        head_weight,
        preferred_element_type=jnp.float32,
    )
    vocab_start = lax.axis_index(("row", "col")) * vocab_width
    request_base = jnp.arange(group_requests, dtype=jnp.int32)[:, None] * NODES
    parent_rows = (request_base + parents).reshape(-1)
    token_cols = tokens.reshape(-1) - vocab_start
    inside = (token_cols >= 0) & (token_cols < vocab_width)
    picked = jnp.where(inside, logits[parent_rows, jnp.clip(token_cols, 0, vocab_width - 1)], 0.0)
    local_max = jnp.max(logits, axis=1)
    local_total = jnp.sum(jnp.exp(logits - local_max[:, None]), axis=1)
    whole_max, whole_total, whole_pick = combined_all(
        (local_max, local_total, picked), ("row", "col"), combine_parts
    )
    log_total = whole_max + jnp.log(whole_total)
    node_ids = jnp.arange(NODES, dtype=jnp.int32)[None, :]
    live_nodes = (node_ids > 0) & (node_ids < counts[:, None])
    node_scores = (whole_pick - log_total[parent_rows]).reshape(group_requests, NODES)
    node_logprob = jnp.where(live_nodes, node_scores, jnp.zeros_like(node_scores))
    last_nodes = jnp.take_along_axis(accepted_path, (accept_count - 1)[:, None], axis=1)[:, 0]
    last_rows = request_base[:, 0] + last_nodes
    next_logprob = logits[last_rows] - log_total[last_rows][:, None]
    own_path = lax.dynamic_slice_in_dim(accepted_path, row_slot * local_requests, local_requests, 0)
    own_accept = lax.dynamic_slice_in_dim(
        accept_count, row_slot * local_requests, local_requests, 0
    )
    fresh_rows = jnp.concatenate([new_keys, new_values], axis=3)
    chosen_rows = jnp.take_along_axis(fresh_rows, own_path[:, :, None, None], axis=1)
    step_ids = jnp.arange(own_path.shape[1], dtype=jnp.int32)
    kept_rows = (step_ids[None, :] < own_accept[:, None])[:, :, None, None]
    accepted_cache = jnp.where(kept_rows, chosen_rows, jnp.zeros_like(chosen_rows))
    return (node_logprob, next_logprob, accepted_cache)


def solution(mesh):
    in_specs = (
        P("req", None),
        P(),
        P("row", "col"),
        P("row", "col", None),
        P("col", "row"),
        P(),
        P(None, ("row", "col")),
        P(("req", "row"), None, "col", None),
        P("req", None),
        P("req"),
        P("req"),
        P("req", None),
        P("req", None),
        P("req"),
    )
    out_specs = (P("req", None), P("req", ("row", "col")), P(("req", "row"), None, "col", None))
    return jax.shard_map(shards, mesh=mesh, in_specs=in_specs, out_specs=out_specs, check_vma=False)
```

profile of v0, /device:TPU:1, one launch (start us, length us, event | category | flops | bytes accessed | tf_op | source)
XLA Modules:
  0.0 367.2 jit_solution(17106997792936549415)
XLA Ops:
  7.2 2.9 copy.31
  10.7 2.5 convert_element_type.107
  13.2 0.8 dynamic_slice.78
  14.0 2.6 fusion.9
  20.8 32.5 %reduce-scatter.3.cloned.1.call-done = f32[64,640]{1,0:T(8,128)} async-done(((f32[512,640]{1,0:T(8,128)}), f32[64,640]{1,0:T(8,128)}) %reduce-scatter.3.cloned.1.call-update) | async-done | bytes 163856 | tf_op jit(solution)/shard_map/reduce_scatter | solution.py:118
  53.4 0.8 slice_bitcast_fusion
  54.7 0.9 slice.77
  56.0 1.0 fusion.49
  57.0 0.7 fusion.2
  57.7 1.4 fusion.5
  59.2 15.9 %all_gather.22 = bf16[512,512]{1,0:T(8,128)(2,1)S(1)} all-gather(bf16[64,512]{1,0:T(8,128)(2,1)S(1)} %copy.37), channel_id=1, replica_groups=mesh['req'=8,'row'=8,'col'=4] {'row'}, dimensions={0}, use_global_device_ids=true | all-gather | bytes 589824 | tf_op jit(solution)/shard_map/all_gather | solution.py:143
  75.1 1.1 fusion.51
  76.4 0.8 dynamic_slice.82
  77.1 20.4 %reduce-scatter.5.cloned.1.call-done = f32[512,64]{0,1:T(8,128)} async-done(((f32[512,256]{0,1:T(8,128)}), f32[512,64]{0,1:T(8,128)}) %reduce-scatter.5.cloned.1.call-update) | async-done | bytes 131088 | tf_op jit(solution)/shard_map/reduce_scatter | solution.py:148
  97.6 1.0 multiply_reduce_fusion.1
  98.6 61.3 %psum.7 = f32[512]{0:T(512)S(1)} all-reduce(f32[512]{0:T(512)S(1)} %multiply_reduce_fusion.1), channel_id=1, replica_groups=mesh['req'=8,'row'=8,'col'=4] {'row','col'}, use_global_device_ids=true, to_apply=%region_7.8 | all-reduce | flops 512 | bytes 4096 | tf_op jit(solution)/shard_map/psum | solution.py:152
  159.8 1.7 multiply_convert_fusion.2
  163.2 0.7 iota_compare_fusion.3
  164.7 0.7 fusion.38
  165.3 47.3 %all-gather.7.cloned.1.call-done = bf16[512,2048]{0,1:T(8,128)(2,1)} async-done(((bf16[512,64]{0,1:T(8,128)(2,1)}), bf16[512,2048]{0,1:T(8,128)(2,1)}) %all-gather.7.cloned.1.call-update) | async-done | bytes 2097168 | tf_op jit(solution)/shard_map/all_gather | solution.py:158
  212.6 5.1 %fusion.50 = (f32[512]{0:T(512)S(1)}, f32[512,1002]{0,1:T(8,128)S(1)}) fusion(bf16[512,2048]{0,1:T(8,128)(2,1)} %all-gather.7.cloned.1.call-done, bf16[2048,1002]{0,1:T(8,128)(2,1)} %param.22), kind=kOutput, calls=%fused_computation.126 | convolution fusion | flops 2101858816 | bytes 8255488 | tf_op jit(solution)/shard_map/dot_general | solution.py:157
  217.7 1.9 copy.38
  219.9 40.7 %all-gather.3 = f32[32,1,512]{2,1,0:T(1,128)S(1)} all-gather(f32[1,1,512]{2,1,0:T(1,128)S(1)} %bitcast.127), channel_id=3, replica_groups=mesh['req'=8,'row'=8,'col'=4] {'row','col'}, dimensions={0}, use_global_device_ids=true | all-gather | bytes 67584 | tf_op jit(solution)/shard_map/all_gather | solution.py:16
  260.7 4.5 %gather_fusion = f32[512]{0:T(512)S(1)} fusion(f32[512,1002]{0,1:T(8,128)S(1)} %get-tuple-element.248, s32[512]{0:T(512)S(1)} %bitcast.108), kind=kCustom, calls=%fused_computation | custom fusion | bytes 8192 | tf_op jit(solution)/shard_map/gather | solution.py:167
  265.2 43.1 %all-gather.4 = f32[32,1,512]{2,1,0:T(1,128)S(1)} all-gather(f32[1,1,512]{2,1,0:T(1,128)S(1)} %select_bitcast_fusion), channel_id=1, replica_groups=mesh['req'=8,'row'=8,'col'=4] {'row','col'}, dimensions={0}, use_global_device_ids=true | all-gather | bytes 67584 | tf_op jit(solution)/shard_map/all_gather | solution.py:16
  308.3 41.7 %all-gather.2 = f32[32,1,512]{2,1,0:T(1,128)S(1)} all-gather(f32[1,1,512]{2,1,0:T(1,128)S(1)} %bitcast.125), channel_id=2, replica_groups=mesh['req'=8,'row'=8,'col'=4] {'row','col'}, dimensions={0}, use_global_device_ids=true | all-gather | bytes 67584 | tf_op jit(solution)/shard_map/all_gather | solution.py:16
  350.0 2.9 while.23
  352.9 2.2 gather_fusion.2
  355.1 0.6 gather_fusion.3
  355.7 3.5 gather_fusion.1
  359.3 0.7 broadcast_subtract_fusion
  360.0 0.7 fusion.34
  (216 shorter events, 9.0 us)
Async XLA Ops:
  7.2 68.0 %copy-start = (bf16[512,256]{1,0:T(8,128)(2,1)S(1)}, bf16[512,256]{1,0:T(8,128)(2,1)}, u32[]{:S(2)}) copy-start(bf16[512,256]{1,0:T(8,128)(2,1)} %param.20) | copy-start | bytes 786436
  7.2 46.2 %reduce-scatter.3.cloned.1.call-start = ((), (), s32[]{:S(2)}) async-start(), calls=%async_computation.2 | async-start | bytes 1474560 | tf_op jit(solution)/shard_map/reduce_scatter | solution.py:118
  10.1 3.9 %copy-start.3 = (bf16[256,512]{1,0:T(8,128)(2,1)S(1)}, bf16[256,512]{1,0:T(8,128)(2,1)}, u32[]{:S(2)}) copy-start(bf16[256,512]{1,0:T(8,128)(2,1)} %param.18) | copy-start | bytes 786436
  10.1 3.9 %copy-start.4 = (bf16[256,1,128]{2,0,1:T(8,128)(2,1)S(1)}, bf16[256,1,128]{2,0,1:T(8,128)(2,1)}, u32[]{:S(2)}) copy-start(bf16[256,1,128]{2,0,1:T(8,128)(2,1)} %param.19) | copy-start | bytes 196612
  10.7 6.0 %copy-start.6 = (s32[8,64]{1,0:T(8,128)S(1)}, s32[8,64]{1,0:T(8,128)}, u32[]{:S(2)}) copy-start(s32[8,64]{1,0:T(8,128)} %param.24) | copy-start | bytes 6148
  10.7 6.9 %copy-start.8 = (s32[8]{0:T(128)S(1)}, s32[8]{0:T(128)}, u32[]{:S(2)}) copy-start(s32[8]{0:T(128)} %param.26) | copy-start | bytes 100
  10.7 8.8 %copy-start.2 = (bf16[1,2048,1,128]{3,1,2,0:T(8,128)(2,1)S(1)}, bf16[1,2048,1,128]{3,1,2,0:T(8,128)(2,1)}, u32[]{:S(2)}) copy-start(bf16[1,2048,1,128]{3,1,2,0:T(8,128)(2,1)} %param.23) | copy-start | bytes 1572868
  16.6 80.9 %reduce-scatter.5.cloned.1.call-start = ((), (), s32[]{:S(2)}) async-start(), calls=%async_computation.3 | async-start | bytes 655360 | tf_op jit(solution)/shard_map/reduce_scatter | solution.py:148
  57.7 103.8 %copy-start.9 = (s32[8]{0:T(128)S(1)}, s32[8]{0:T(128)}, u32[]{:S(2)}) copy-start(s32[8]{0:T(128)} %param.29) | copy-start | bytes 100
  57.7 104.4 %copy-start.5 = (s32[8,64]{1,0:T(8,128)S(1)}, s32[8,64]{1,0:T(8,128)}, u32[]{:S(2)}) copy-start(s32[8,64]{1,0:T(8,128)} %param.27) | copy-start | bytes 6148
  57.7 104.8 %copy-start.1 = (s32[8,8]{1,0:T(8,128)S(1)}, s32[8,8]{1,0:T(8,128)}, u32[]{:S(2)}) copy-start(s32[8,8]{1,0:T(8,128)} %param.28) | copy-start | bytes 772
  76.3 136.3 %all-gather.7.cloned.1.call-start = ((), (), s32[]{:S(2)}) async-start(), calls=%async_computation.4 | async-start | bytes 2162688 | tf_op jit(solution)/shard_map/all_gather | solution.py:158
  219.6 140.4 %copy-start.7 = (s32[8]{0:T(128)S(1)}, s32[8]{0:T(128)}, u32[]{:S(2)}) copy-start(s32[8]{0:T(128)} %param.25) | copy-start | bytes 100
Sparse Core Ops, SparseCore 0:
  16.7 36.5 reduce-scatter.2
  76.4 21.0 reduce-scatter.4
  161.7 50.9 all-gather.6
where the time goes:
time: 368 us; the launch traced here: 367 us
  blocking collectives  203 us (55%)
  waiting for transfers between devices  100 us (27%)
  local copies, waits for them, and re-layouts  23.3 us (6%)
  between operations  15.5 us (4%)
  matrix products  12.4 us (3%)
  other arithmetic  11.8 us (3%)
    all_gather x3, blocking collectives, combined_all(): everything = jax.tree.map(lambda part: lax.all_gather(part, axis), value)  125 us
    psum x1, blocking collectives, shards(): squares = lax.psum(jnp.sum(residual * residual, axis=1), ('row', 'col'))  61.3 us
    all_gather x1, waiting for transfers between devices, shards(): lax.all_gather(normed_out, ('row', 'col'), axis=1, tiled=True)  47.3 us
    reduce_scatter x1, waiting for transfers between devices, shards(): lax.psum_scatter(jnp.dot(normed, joint_weight, preferred_element_type=jnp...  32.5 us
    reduce_scatter x1, waiting for transfers between devices, shards(): lax.psum_scatter(head_terms, 'col', scatter_dimension=1, tiled=True)  20.4 us
    all_gather x1, blocking collectives, shards(): lax.all_gather(attended, 'row', axis=0, tiled=True)  15.9 us
  transfers between devices with their start and end apart: 3, of which 3 were waited for; matrix products, arithmetic and copies ran while one was open for 2% of the time, Pallas kernels for 0%

commit v1 on v0

v1 whole, which is shorter than its diff:
```python
import functools

import jax
import jax.numpy as jnp
import numpy as np
from jax import lax
from jax.experimental import pallas as pl
from jax.experimental.pallas import tpu as pltpu
from jax.sharding import PartitionSpec as P

D = 2048
NODES = 64
WIN = 2048
VW = 1002
F32 = jnp.float32
BF16 = jnp.bfloat16
EPS = 1e-5
NEAR_FIRST = (1, 3, 2)


def dot(a, b):
    return jnp.dot(a, b, preferred_element_type=F32)


def dot_nt(a, b):
    return lax.dot_general(a, b, (((1,), (1,)), ((), ())), preferred_element_type=F32)


def body(
    hid, again, wq, wkv, wo, fgain, wh, cache, par, tok, path, freq,
    counts, lengths, accepts,
    out_node, out_next, out_cache,
    H, AG, W1, WO, FG, WV, C, PAR, TOK, PATH, FREQ,
    PF, NB, send1, recv1, A, PO, send2, recv2, G, ACC, IG2,
    st1, st2, nx_send, nx_recv,
    lsem, psend, precv, s1s, s1r, as_, ar, s2s, s2r, gas, gar, gbs, gbr,
    t1s, t1r, t2s, t2r, nxs, nxr,
):
    r = lax.axis_index("row")
    y = lax.axis_index("col")
    x = lax.div(r, 2)
    k = lax.rem(r, 2)
    other = 1 - k
    me = r

    def dev(x2, k2, y2):
        return {"row": 2 * x2 + k2, "col": y2}

    def ring(v, d):
        return lax.rem(v + d, 4)

    def remote(src, dst, ssem, rsem, where):
        return pltpu.make_async_remote_copy(
            src_ref=src, dst_ref=dst, send_sem=ssem, recv_sem=rsem,
            device_id=where, device_id_type=pl.DeviceIdType.MESH,
        )

    def rows(i, n=64):
        return pl.ds(pl.multiple_of(i * n, n), n)

    barrier = pltpu.get_barrier_semaphore()
    peers = [dev(x, other, y)]
    for d in (1, 2, 3):
        peers += [dev(ring(x, d), k, y), dev(ring(x, d), other, y), dev(x, k, ring(y, d))]
    for p in peers:
        pl.semaphore_signal(barrier, inc=1, device_id=p, device_id_type=pl.DeviceIdType.MESH)

    local = []

    def fetch(src, dst):
        copy = pltpu.make_async_copy(src, dst, lsem.at[len(local)])
        copy.start()
        local.append(copy)
        return copy

    h_copies = [fetch(hid.at[pl.ds(pl.multiple_of((2 * q + k) * 64, 64), 64)], H.at[pl.ds(64 * q, 64)]) for q in range(4)]
    small = [fetch(a, b) for a, b in ((again, AG), (par, PAR), (path, PATH), (freq, FREQ))]
    half_rows = rows(k, 256)
    w1_copies = [fetch(wq, W1.at[half_rows, pl.ds(0, 512)]), fetch(wkv, W1.at[half_rows, pl.ds(512, 128)])]
    c_copy = fetch(cache, C)
    late = [fetch(fgain, FG), fetch(tok, TOK)]
    wo_copy = fetch(wo, WO.at[:, half_rows])
    wh_copies = []
    for xx in range(4):
        for h in range(2):
            wh_copies.append(fetch(wh.at[:, pl.ds(512 * xx + 256 * h, 256)], WV.at[0, h, :, pl.ds(256 * xx, 256)]))

    pl.semaphore_wait(barrier, len(peers))

    partner = dev(x, other, y)
    swaps = []

    def swap(src, dst):
        copy = remote(src, dst, psend.at[len(swaps)], precv.at[len(swaps)], partner)
        copy.start()
        swaps.append(copy)
        return copy

    w1_swaps = [swap(wq, W1.at[half_rows, pl.ds(0, 512)]), swap(wkv, W1.at[half_rows, pl.ds(512, 128)])]
    wo_swap = swap(wo, WO.at[:, half_rows])
    wh_swaps = []
    for xx in range(4):
        for h in range(2):
            wh_swaps.append(swap(wh.at[:, pl.ds(512 * xx + 256 * h, 256)], WV.at[1, h, :, pl.ds(256 * xx, 256)]))

    for c in small:
        c.wait()
    own_cols = pl.ds(pl.multiple_of(512 * x, 512), 512)
    gain_row = AG[:, own_cols]
    for q in range(4):
        h_copies[q].wait()
        wide = H[pl.ds(64 * q, 64), :].astype(F32)
        inv = lax.rsqrt(jnp.sum(wide * wide, axis=1, keepdims=True) * (1.0 / D) + EPS)
        part = H[pl.ds(64 * q, 64), own_cols].astype(F32)
        NB[pl.ds(64 * q, 64), :] = (part * inv * gain_row).astype(BF16)
    for c in w1_copies:
        c.wait()
    for c in w1_swaps:
        c.wait_recv()
    PF[...] = dot(NB[...], W1[...])
    first = []
    for d in NEAR_FIRST:
        q = ring(x, d)
        send1[d] = PF[rows(q), :].astype(BF16)
        copy = remote(send1.at[d], recv1.at[d], s1s.at[d], s1r.at[d], dev(q, k, y))
        copy.start()
        first.append(copy)

    lane64 = lax.broadcasted_iota(jnp.int32, (64, 64), 1)
    sub64 = lax.broadcasted_iota(jnp.int32, (64, 64), 0)
    eye = lane64 == sub64
    eye8 = lax.broadcasted_iota(jnp.int32, (8, 8), 0) == lax.broadcasted_iota(jnp.int32, (8, 8), 1)

    def column(row_values):
        return jnp.sum(jnp.where(eye, row_values, 0), axis=1, keepdims=True)

    def parent_column(b):
        return column(PAR[pl.ds(b, 1), :])

    def gather_matrix(b, parents_col):
        path_row = PATH[pl.ds(b, 1), :]
        lane8 = lax.broadcasted_iota(jnp.int32, (1, 8), 1)
        last = jnp.sum(jnp.where(lane8 == accepts[b] - 1, path_row, 0), axis=1, keepdims=True)
        source = jnp.where(sub64[:, :1] == 0, last, parents_col)
        return jnp.where(source == lane64, 1.0, 0.0).astype(BF16)

    parents_col = parent_column(me)
    reach = jnp.where(eye | ((parents_col == lane64) & (sub64 > 0)), 1.0, 0.0)
    for _ in range(6):
        half = reach.astype(BF16)
        reach = jnp.minimum(dot(half, half), 1.0)
    depth = jnp.sum(reach, axis=1, keepdims=True) - 1.0
    length = lengths[me]
    angles = (length.astype(F32) + depth) * FREQ[...]
    cosine = jnp.cos(angles)
    sine = jnp.sin(angles)
    closed = jnp.maximum(depth.astype(jnp.int32), WIN - 1 - length)
    gather_own = gather_matrix(me, parents_col)
    gather_y = gather_matrix(2 * y + k, parent_column(2 * y + k))
    hid_y = dot(gather_y, H[rows(y), own_cols])

    lane = lax.broadcasted_iota(jnp.int32, (64, 128), 1)
    front = lax.rem(lane, 64) < 32
    low = lane < 64

    def rotated(u):
        turned = jnp.where(front, -pltpu.roll(u, 96, 1), pltpu.roll(u, 32, 1))
        return u * cosine + turned * sine

    eye256 = lax.broadcasted_iota(jnp.int32, (256, 256), 0) == lax.broadcasted_iota(jnp.int32, (256, 256), 1)

    def as_row(col):
        return jnp.sum(jnp.where(eye256, col, jnp.zeros_like(col)), axis=0, keepdims=True)

    c_copy.wait()
    for c in late:
        c.wait()
    IG2[...] = 1.0 / (FG[...] * FG[...])
    token_cols = [column(TOK[pl.ds(2 * q + k, 1), :]) for q in range(4)]
    token_row = as_row(jnp.concatenate(token_cols, axis=0))

    for copy in first:
        copy.wait_recv()
    raw = PF[rows(x), :] + recv1[1].astype(F32) + recv1[2].astype(F32) + recv1[3].astype(F32)
    pair = raw[:, 512:640]
    fresh = jnp.where(low, rotated(pair), pair).astype(BF16)
    path_row = PATH[pl.ds(me, 1), :]
    path_col = jnp.sum(jnp.where(eye8, path_row, 0), axis=1, keepdims=True)
    lane8x64 = lax.broadcasted_iota(jnp.int32, (8, 64), 1)
    sub8x64 = lax.broadcasted_iota(jnp.int32, (8, 64), 0)
    chosen = jnp.where((path_col == lane8x64) & (sub8x64 < accepts[me]), 1.0, 0.0).astype(BF16)
    out_cache[...] = dot(chosen, fresh).astype(BF16)

    slot = lax.broadcasted_iota(jnp.int32, (256, WIN), 1)
    closed4 = jnp.concatenate([closed] * 4, axis=0)
    reach4 = jnp.concatenate([reach] * 4, axis=0) > 0.5
    spread = []
    for hc in range(2):
        stack = []
        for j in range(2):
            at = 256 * hc + 128 * j
            turned = rotated(raw[:, at : at + 128]).astype(BF16).astype(F32) * 0.125
            stack.append(jnp.where(low, turned, 0.0))
            stack.append(jnp.where(low, pltpu.roll(turned, 64, 1), 0.0))
        queries = jnp.concatenate(stack, axis=0).astype(BF16)
        scores = jnp.where(slot > closed4, dot_nt(queries, C[...]), -jnp.inf)
        scores_new = jnp.where(reach4, dot_nt(queries, fresh), -jnp.inf)
        top = jnp.maximum(jnp.max(scores, axis=1, keepdims=True), jnp.max(scores_new, axis=1, keepdims=True))
        w = jnp.exp(scores - top)
        w_new = jnp.exp(scores_new - top)
        total = jnp.sum(w, axis=1, keepdims=True) + jnp.sum(w_new, axis=1, keepdims=True)
        o = (dot(w.astype(BF16), C[...]) + dot(w_new.astype(BF16), fresh)) / total
        blocks = [
            jnp.where(low, pltpu.roll(o[128 * j : 128 * j + 64], 64, 1), o[128 * j + 64 : 128 * j + 128])
            for j in range(2)
        ]
        attended = jnp.concatenate(blocks, axis=1).astype(BF16)
        A[hc, rows(x), :] = dot(gather_own, attended).astype(BF16)
        for d in NEAR_FIRST:
            at = A.at[hc, rows(x)]
            copy = remote(at, at, as_.at[hc, d], ar.at[hc, d], dev(ring(x, d), k, y))
            copy.start()
            spread.append(copy)

    wo_copy.wait()
    wo_swap.wait_recv()
    for copy in spread:
        copy.wait_recv()
    second = {}
    for h in range(2):
        cols = pl.ds(256 * h, 256)
        PO[h] = dot(A[0], WO[pl.ds(0, 256), cols]) + dot(A[1], WO[pl.ds(256, 256), cols])
        for d in NEAR_FIRST:
            q = ring(y, d)
            send2[h, d] = PO[h, rows(q), :].astype(BF16)
            copy = remote(send2.at[h, d], recv2.at[h, d], s2s.at[h, d], s2r.at[h, d], dev(x, k, q))
            copy.start()
            second[h, d] = copy

    def piece(h, xx, yy):
        return G.at[h, rows(yy), pl.ds(pl.multiple_of(256 * xx, 256), 256)]

    def stage_one_copy(h, d):
        at = piece(h, x, y)
        where = dev(x, k, ring(y, d)) if h == 0 else dev(ring(x, d), k, y)
        return remote(at, at, gas.at[h, d], gar.at[h, d], where)

    def stage_two_copy(h, e, d):
        if h == 0:
            at = piece(0, x, ring(y, 4 - d))
            where = dev(ring(x, e), k, y)
        else:
            at = piece(1, ring(x, 4 - d), y)
            where = dev(x, k, ring(y, e))
        return remote(at, at, gbs.at[h, e, d], gbr.at[h, e, d], where)

    stage_one, stage_two = {}, {}
    for h in range(2):
        for d in NEAR_FIRST:
            second[h, d].wait_recv()
        res = (
            PO[h, rows(y), :]
            + recv2[h, 1].astype(F32) + recv2[h, 2].astype(F32) + recv2[h, 3].astype(F32)
            + hid_y[:, 256 * h : 256 * h + 256]
        )
        gain = FG[:, pl.ds(pl.multiple_of(512 * x + 256 * h, 256), 256)]
        G[h, rows(y), pl.ds(pl.multiple_of(256 * x, 256), 256)] = (res * gain).astype(BF16)
        for d in NEAR_FIRST:
            stage_one[h, d] = stage_one_copy(h, d)
            stage_one[h, d].start()
        for e in NEAR_FIRST:
            stage_two[h, e, 0] = stage_two_copy(h, e, 0)
            stage_two[h, e, 0].start()
    for d in NEAR_FIRST:
        for h in range(2):
            stage_one[h, d].wait_recv()
            for e in NEAR_FIRST:
                stage_two[h, e, d] = stage_two_copy(h, e, d)
                stage_two[h, e, d].start()

    for c in wh_copies:
        c.wait()
    for c in wh_swaps:
        c.wait_recv()

    def squares(h, xx):
        u = G[h, :, pl.ds(pl.multiple_of(256 * xx, 256), 256)].astype(F32)
        scale = IG2[:, pl.ds(pl.multiple_of(512 * xx + 256 * h, 256), 256)]
        return jnp.sum(u * u * scale, axis=1, keepdims=True)

    sq = jnp.zeros((256, 1), F32)
    for e in (0,) + NEAR_FIRST:
        xx = ring(x, 4 - e)
        if e:
            for d in range(4):
                stage_two[0, e, d].wait_recv()
        sq = sq + squares(0, xx)
        cols = rows(xx, 256)
        rhs = G[0, :, cols]

        def add_chunk(s, carry, rhs=rhs, cols=cols, begin=(e == 0)):
            term = dot_nt(WV[s, 0, :, cols], rhs)
            ACC[s] = term if begin else ACC[s] + term
            return carry

        lax.fori_loop(0, 2, add_chunk, 0)
    for e in NEAR_FIRST:
        for d in range(4):
            stage_two[1, e, d].wait_recv()
    for xx in range(4):
        sq = sq + squares(1, xx)
    inv = as_row(lax.rsqrt(sq * (1.0 / D) + EPS))

    def finish(s, top):
        t = (ACC[s] + dot_nt(WV[s, 1], G[1])) * inv
        ACC[s] = t
        return jnp.maximum(top, jnp.max(t, axis=0, keepdims=True))

    top = lax.fori_loop(0, 2, finish, jnp.full((1, 256), -jnp.inf, F32))
    vocab = lax.broadcasted_iota(jnp.int32, (VW, 256), 0)

    def totals(s, carry):
        total, pick = carry
        t = ACC[s]
        holder = jnp.where(s == 0, k, other)
        start = ((2 * x + holder) * 4 + y) * VW
        total = total + jnp.sum(jnp.exp(t - top), axis=0, keepdims=True)
        pick = pick + jnp.sum(jnp.where(vocab == token_row - start, t, 0.0), axis=0, keepdims=True)
        return total, pick

    zero = jnp.zeros((1, 256), F32)
    total, pick = lax.fori_loop(0, 2, totals, (zero, zero))
    st1[0] = jnp.concatenate([top, total, pick, jnp.zeros((5, 256), F32)], axis=0)
    third = []
    for d in NEAR_FIRST:
        copy = remote(st1.at[0], st1.at[d], t1s.at[d], t1r.at[d], dev(x, k, ring(y, d)))
        copy.start()
        third.append(copy)

    first_of = lax.broadcasted_iota(jnp.int32, (8, 256), 0) * 64 == lax.broadcasted_iota(jnp.int32, (8, 256), 1)
    first_of = jnp.where(first_of, 1.0, 0.0)

    def last_rows(s):
        return lax.dot_general(
            first_of, ACC[s], (((1,), (1,)), ((), ())),
            precision=lax.Precision.HIGHEST, preferred_element_type=F32,
        )

    nx_send[...] = last_rows(1)
    nx = remote(nx_send, nx_recv, nxs, nxr, partner)
    nx.start()
    own_next = last_rows(0)

    def combine(parts):
        tops = [p[0:1] for p in parts]
        m = functools.reduce(jnp.maximum, tops)
        total = sum(p[1:2] * jnp.exp(t - m) for p, t in zip(parts, tops))
        pick = sum(p[2:3] for p in parts)
        return m, total, pick

    for copy in third:
        copy.wait_recv()
    m, total4, pick4 = combine([st1[d] for d in range(4)])
    st2[me] = jnp.concatenate([m, total4, pick4, jnp.zeros((5, 256), F32)], axis=0)
    fourth = []
    for i, (d, flip) in enumerate(((0, 1), (1, 0), (1, 1), (3, 0), (3, 1), (2, 0), (2, 1))):
        copy = remote(
            st2.at[me], st2.at[me], t2s.at[i], t2r.at[i],
            dev(ring(x, d), other if flip else k, y),
        )
        copy.start()
        fourth.append(copy)
    nx.wait_recv()
    for copy in fourth:
        copy.wait_recv()
    lane1 = lax.broadcasted_iota(jnp.int32, (1, 64), 1)
    for plane in range(2):
        m, total4, pick4 = combine([st2[2 * xx + plane] for xx in range(4)])
        log_total = m + jnp.log(total4)
        score = pick4 - log_total
        for q in range(4):
            b = 2 * q + plane
            at = slice(64 * q, 64 * q + 64)
            live = (lane1 > 0) & (lane1 < counts[b])
            out_node[pl.ds(b, 1), :] = jnp.where(live, score[:, at], 0.0)
            row = jnp.where(k == plane, own_next[q : q + 1], nx_recv[pl.ds(q, 1), :])
            out_next[pl.ds(b, 1), :] = row - log_total[:, 64 * q : 64 * q + 1]

    for copy in swaps + first + spread + list(second.values()) + list(stage_one.values()):
        copy.wait_send()
    for copy in list(stage_two.values()) + third + fourth + [nx]:
        copy.wait_send()


def shards(
    hidden, attention_gain, query_weight, key_value_weight, output_weight, final_gain, head_weight,
    key_value_cache, parents, counts, lengths, tokens, accepted_path, accept_count,
):
    half = 32
    freq = 10000.0 ** (-np.arange(half, dtype=np.float64) / half)
    freq = jnp.asarray(np.tile(freq, 4)[None], F32)
    anywhere = pl.BlockSpec(memory_space=pl.ANY)
    scalars = pl.BlockSpec(memory_space=pltpu.SMEM)
    vmem = pl.BlockSpec(memory_space=pltpu.VMEM)
    dma = pltpu.SemaphoreType.DMA
    node, following, cache_rows = pl.pallas_call(
        body,
        out_shape=(
            jax.ShapeDtypeStruct((8, NODES), F32),
            jax.ShapeDtypeStruct((8, VW), F32),
            jax.ShapeDtypeStruct((8, 128), BF16),
        ),
        in_specs=[anywhere] * 12 + [scalars] * 3,
        out_specs=(vmem, vmem, vmem),
        scratch_shapes=[
            pltpu.VMEM((256, D), BF16),
            pltpu.VMEM((1, D), F32),
            pltpu.VMEM((512, 640), BF16),
            pltpu.VMEM((512, 512), BF16),
            pltpu.VMEM((1, D), F32),
            pltpu.VMEM((2, 2, VW, 1024), BF16),
            pltpu.VMEM((WIN, 128), BF16),
            pltpu.VMEM((8, NODES), jnp.int32),
            pltpu.VMEM((8, NODES), jnp.int32),
            pltpu.VMEM((8, 8), jnp.int32),
            pltpu.VMEM((1, 128), F32),
            pltpu.VMEM((256, 640), F32),
            pltpu.VMEM((256, 512), BF16),
            pltpu.VMEM((4, 64, 640), BF16),
            pltpu.VMEM((4, 64, 640), BF16),
            pltpu.VMEM((2, 256, 256), BF16),
            pltpu.VMEM((2, 256, 256), F32),
            pltpu.VMEM((2, 4, 64, 256), BF16),
            pltpu.VMEM((2, 4, 64, 256), BF16),
            pltpu.VMEM((2, 256, 1024), BF16),
            pltpu.VMEM((2, VW, 256), F32),
            pltpu.VMEM((1, D), F32),
            pltpu.VMEM((4, 8, 256), F32),
            pltpu.VMEM((8, 8, 256), F32),
            pltpu.VMEM((8, VW), F32),
            pltpu.VMEM((8, VW), F32),
            dma((24,)), dma((12,)), dma((12,)),
            dma((4,)), dma((4,)), dma((2, 4)), dma((2, 4)), dma((2, 4)), dma((2, 4)),
            dma((2, 4)), dma((2, 4)), dma((2, 4, 4)), dma((2, 4, 4)),
            dma((4,)), dma((4,)), dma((8,)), dma((8,)), dma(()), dma(()),
        ],
        compiler_params=pltpu.CompilerParams(
            collective_id=0, has_side_effects=True, vmem_limit_bytes=60 * 1024 * 1024
        ),
        name="verify",
    )(
        hidden,
        attention_gain.reshape(1, D),
        query_weight,
        key_value_weight.reshape(256, 128),
        output_weight,
        final_gain.reshape(1, D),
        head_weight.T,
        key_value_cache.reshape(WIN, 128),
        parents,
        tokens,
        accepted_path,
        freq,
        counts,
        lengths,
        accept_count,
    )
    return node, following, cache_rows.reshape(1, 8, 1, 128)


def solution(mesh):
    in_specs = (
        P("req", None),
        P(),
        P("row", "col"),
        P("row", "col", None),
        P("col", "row"),
        P(),
        P(None, ("row", "col")),
        P(("req", "row"), None, "col", None),
        P("req", None),
        P("req"),
        P("req"),
        P("req", None),
        P("req", None),
        P("req"),
    )
    out_specs = (P("req", None), P("req", ("row", "col")), P(("req", "row"), None, "col", None))
    return jax.shard_map(shards, mesh=mesh, in_specs=in_specs, out_specs=out_specs, check_vma=False)
```

time: 368 us -> 53.6 us (0.15)
  blocking collectives: 203 us -> 0 us
  waiting for transfers between devices: 100 us -> 0 us
  Pallas kernels: 0 us -> 48.8 us
  local copies, waits for them, and re-layouts: 23.3 us -> 3.88 us
  between operations: 15.5 us -> 0.65 us
  matrix products: 12.4 us -> 0 us
  other arithmetic: 11.8 us -> 0 us
    all_gather x4 -> x0, blocking collectives: 141 us -> none  [the longest x3 125 us: combined_all(): everything = jax.tree.map(lambda part: lax.all_gather(part, axis), value)]
    psum x1 -> x0, blocking collectives: 61.3 us -> none  [shards(): squares = lax.psum(jnp.sum(residual * residual, axis=1), ('row', 'col'))]
    reduce_scatter x2 -> x0, waiting for transfers between devices: 53 us -> none  [the longest x1 32.5 us: shards(): lax.psum_scatter(jnp.dot(normed, joint_weight, preferred_element_type=jnp...]
    pallas_call x0 -> x1, Pallas kernels: none -> 48.8 us  [shards(): pl.pallas_call(body, out_shape=(jax.ShapeDtypeStruct((8, NODES), F32), ja...]
    all_gather x1 -> x0, waiting for transfers between devices: 47.3 us -> none  [shards(): lax.all_gather(normed_out, ('row', 'col'), axis=1, tiled=True)]
    dot_general x12 -> x0, matrix products: 12.4 us -> none  [the longest x1 5.11 us: shards(): jnp.dot(lax.all_gather(normed_out, ('row', 'col'), axis=1, tiled=True), h...]
    gather x6 -> x0, local copies, waits for them, and re-layouts: 12.1 us -> none  [the longest x1 4.55 us: shards(): logits[parent_rows, jnp.clip(token_cols, 0, vocab_width - 1)]]
    convert_element_type x2 -> x0, other arithmetic: 4.2 us -> none  [the longest x1 2.53 us: shards(): widened = hidden.astype(jnp.float32)]
  transfers between devices with their start and end apart: 3 -> 0, of which waited for: 3 -> 0; matrix products, arithmetic and copies ran while one was open for 2% -> 0% of each run, Pallas kernels for 0% -> 0%
where the time goes in v1:
time: 53.6 us; the launch traced here: 53.4 us
  Pallas kernels  48.8 us (91%)
  local copies, waits for them, and re-layouts  3.88 us (7%)
  between operations  0.65 us (1%)
    pallas_call x1, Pallas kernels, shards(): pl.pallas_call(body, out_shape=(jax.ShapeDtypeStruct((8, NODES), F32), ja...  48.8 us
    unnamed x3, local copies, waits for them, and re-layouts  3.88 us

profile of v1, /device:TPU:1, one launch (start us, length us, event | category | flops | bytes accessed | tf_op | source)
XLA Modules:
  0.0 53.4 jit_solution(7267532290139561596)
XLA Ops:
  0.6 48.8 %verify.1 = (f32[8,64]{1,0:T(8,128)}, f32[8,1002]{1,0:T(8,128)}, bf16[8,128]{1,0:T(8,128)(2,1)}) custom-call(bf16[512,2048]{1,0:T(8,128)(2,1)} %hid.1, f32[1,2048]{1,0:T(1,128)} %bitcast.9, bf16[256,512]{1,0:T(8,128)(2,1)} %wq.1, bf16[256,128]{1,0:T(8,128)(2,1)} %bitcast.8, bf16[512,256]{1,0:T(8,128)(2,1)} %wo.1, f32[1,2048]{1,0:T(1,128)} %bitcast.10, ...), custom_call_target="tpu_custom_call" | custom-call | tf_op jit(solution)/shard_map/verify/pallas_call | solution.py:406
  49.5 1.3 %copy.21 = f32[8,64]{1,0:T(8,128)} copy(f32[8,64]{1,0:T(8,128)} %get-tuple-element.12) | data formatting | bytes 4096
  50.8 1.4 %copy.22 = f32[8,1002]{1,0:T(8,128)} copy(f32[8,1002]{1,0:T(8,128)} %get-tuple-element.13) | data formatting | bytes 64128
  52.1 1.2 %copy.23 = bf16[1,8,1,128]{3,1,2,0:T(8,128)(2,1)} copy(bf16[1,8,1,128]{3,1,2,0:T(8,128)(2,1)} %bitcast.11) | data formatting | bytes 4096

commit v2 on v1

--- a/solution.py
+++ b/solution.py
@@ -16,6 +16,7 @@
 BF16 = jnp.bfloat16
 EPS = 1e-5
 NEAR_FIRST = (1, 3, 2)
+FAR_FIRST = (2, 1, 3, 0)
 
 
 def dot(a, b):
@@ -31,10 +32,9 @@
     counts, lengths, accepts,
     out_node, out_next, out_cache,
     H, AG, W1, WO, FG, WV, C, PAR, TOK, PATH, FREQ,
-    PF, NB, send1, recv1, A, PO, send2, recv2, G, ACC, IG2,
-    st1, st2, nx_send, nx_recv,
-    lsem, psend, precv, s1s, s1r, as_, ar, s2s, s2r, gas, gar, gbs, gbr,
-    t1s, t1r, t2s, t2r, nxs, nxr,
+    PF, NB, send1, recv1, EQ, AS, AR, G, ACC, IG2, ST, nx_send, nx_recv,
+    lsem, psend, precv, wys, wyr, wps, wpr, s1s, s1r, axs, axr,
+    gas, gar, gbs, gbr, sts, str_, nxs, nxr,
 ):
     r = lax.axis_index("row")
     y = lax.axis_index("col")
@@ -59,9 +59,8 @@
         return pl.ds(pl.multiple_of(i * n, n), n)
 
     barrier = pltpu.get_barrier_semaphore()
-    peers = [dev(x, other, y)]
-    for d in (1, 2, 3):
-        peers += [dev(ring(x, d), k, y), dev(ring(x, d), other, y), dev(x, k, ring(y, d))]
+    everyone = [(dx, dy, flip) for dx in FAR_FIRST for dy in FAR_FIRST for flip in (0, 1) if dx or dy or flip]
+    peers = [dev(ring(x, dx), other if flip else k, ring(y, dy)) for dx, dy, flip in everyone]
     for p in peers:
         pl.semaphore_signal(barrier, inc=1, device_id=p, device_id_type=pl.DeviceIdType.MESH)
 
@@ -79,7 +78,11 @@
     w1_copies = [fetch(wq, W1.at[half_rows, pl.ds(0, 512)]), fetch(wkv, W1.at[half_rows, pl.ds(512, 128)])]
     c_copy = fetch(cache, C)
     late = [fetch(fgain, FG), fetch(tok, TOK)]
-    wo_copy = fetch(wo, WO.at[:, half_rows])
+
+    def wo_piece(hc, yy):
+        return WO.at[hc, rows(yy, 256), half_rows]
+
+    wo_copies = [fetch(wo.at[pl.ds(256 * hc, 256)], wo_piece(hc, y)) for hc in range(2)]
     wh_copies = []
     for xx in range(4):
         for h in range(2):
@@ -97,7 +100,13 @@
         return copy
 
     w1_swaps = [swap(wq, W1.at[half_rows, pl.ds(0, 512)]), swap(wkv, W1.at[half_rows, pl.ds(512, 128)])]
-    wo_swap = swap(wo, WO.at[:, half_rows])
+    wo_swaps = [swap(wo.at[pl.ds(256 * hc, 256)], wo_piece(hc, y)) for hc in range(2)]
+    wo_gathers = {}
+    for d in NEAR_FIRST:
+        for hc in range(2):
+            copy = remote(wo.at[pl.ds(256 * hc, 256)], wo_piece(hc, y), wys.at[hc, d], wyr.at[hc, d], dev(x, k, ring(y, d)))
+            copy.start()
+            wo_gathers[hc, d] = copy
     wh_swaps = []
     for xx in range(4):
         for h in range(2):
@@ -156,8 +165,11 @@
     sine = jnp.sin(angles)
     closed = jnp.maximum(depth.astype(jnp.int32), WIN - 1 - length)
     gather_own = gather_matrix(me, parents_col)
-    gather_y = gather_matrix(2 * y + k, parent_column(2 * y + k))
-    hid_y = dot(gather_y, H[rows(y), own_cols])
+    hid_parts = []
+    for q in range(4):
+        EQ[q] = gather_matrix(2 * q + k, parent_column(2 * q + k))
+        hid_parts.append(dot(EQ[q, rows(y, 16), :], H[pl.ds(64 * q, 64), own_cols]))
+    hid_y = jnp.concatenate(hid_parts, axis=0)
 
     lane = lax.broadcasted_iota(jnp.int32, (64, 128), 1)
     front = lax.rem(lane, 64) < 32
@@ -194,7 +206,7 @@
     slot = lax.broadcasted_iota(jnp.int32, (256, WIN), 1)
     closed4 = jnp.concatenate([closed] * 4, axis=0)
     reach4 = jnp.concatenate([reach] * 4, axis=0) > 0.5
-    spread = []
+    spread = ([], [])
     for hc in range(2):
         stack = []
         for j in range(2):
@@ -215,30 +227,38 @@
             for j in range(2)
         ]
         attended = jnp.concatenate(blocks, axis=1).astype(BF16)
-        A[hc, rows(x), :] = dot(gather_own, attended).astype(BF16)
-        for d in NEAR_FIRST:
-            at = A.at[hc, rows(x)]
-            copy = remote(at, at, as_.at[hc, d], ar.at[hc, d], dev(ring(x, d), k, y))
+        AS[hc] = dot(gather_own, attended).astype(BF16)
+        for dx in FAR_FIRST:
+            for dy in FAR_FIRST:
+                if dx or dy:
+                    to_y = ring(y, dy)
+                    copy = remote(
+                        AS.at[hc, rows(to_y, 16)], AR.at[hc, x, :, rows(y, 256)],
+                        axs.at[hc, dx, dy], axr.at[hc, dx, dy], dev(ring(x, dx), k, to_y),
+                    )
+                    copy.start()
+                    spread[hc].append(copy)
+        AR[hc, x, :, rows(y, 256)] = AS[hc, rows(y, 16), :]
+
+    wo_forwards = []
+    for d in NEAR_FIRST:
+        for hc in range(2):
+            wo_gathers[hc, d].wait_recv()
+            at = wo_piece(hc, ring(y, 4 - d))
+            copy = remote(at, at, wps.at[hc, d], wpr.at[hc, d], partner)
             copy.start()
-            spread.append(copy)
-
-    wo_copy.wait()
-    wo_swap.wait_recv()
-    for copy in spread:
-        copy.wait_recv()
-    second = {}
-    for h in range(2):
-        cols = pl.ds(256 * h, 256)
-        PO[h] = dot(A[0], WO[pl.ds(0, 256), cols]) + dot(A[1], WO[pl.ds(256, 256), cols])
-        for d in NEAR_FIRST:
-            q = ring(y, d)
-            send2[h, d] = PO[h, rows(q), :].astype(BF16)
-            copy = remote(send2.at[h, d], recv2.at[h, d], s2s.at[h, d], s2r.at[h, d], dev(x, k, q))
-            copy.start()
-            second[h, d] = copy
-
+            wo_forwards.append(copy)
+    for c in wo_copies:
+        c.wait()
+    for c in wo_swaps + wo_forwards:
+        c.wait_recv()
+    res = hid_y
+    for hc in range(2):
+        for copy in spread[hc]:
+            copy.wait_recv()
+        res = res + dot(AR[hc].reshape(64, 1024), WO[hc])
     def piece(h, xx, yy):
-        return G.at[h, rows(yy), pl.ds(pl.multiple_of(256 * xx, 256), 256)]
+        return G.at[h, :, rows(yy, 16), rows(xx, 256)]
 
     def stage_one_copy(h, d):
         at = piece(h, x, y)
@@ -256,18 +276,13 @@
 
     stage_one, stage_two = {}, {}
     for h in range(2):
-        for d in NEAR_FIRST:
-            second[h, d].wait_recv()
-        res = (
-            PO[h, rows(y), :]
-            + recv2[h, 1].astype(F32) + recv2[h, 2].astype(F32) + recv2[h, 3].astype(F32)
-            + hid_y[:, 256 * h : 256 * h + 256]
-        )
         gain = FG[:, pl.ds(pl.multiple_of(512 * x + 256 * h, 256), 256)]
-        G[h, rows(y), pl.ds(pl.multiple_of(256 * x, 256), 256)] = (res * gain).astype(BF16)
+        part = (res[:, 256 * h : 256 * h + 256] * gain).astype(BF16)
+        G[h, :, rows(y, 16), rows(x, 256)] = part.reshape(4, 16, 256)
         for d in NEAR_FIRST:
             stage_one[h, d] = stage_one_copy(h, d)
             stage_one[h, d].start()
+    for h in range(2):
         for e in NEAR_FIRST:
             stage_two[h, e, 0] = stage_two_copy(h, e, 0)
             stage_two[h, e, 0].start()
@@ -284,7 +299,7 @@
         c.wait_recv()
 
     def squares(h, xx):
-        u = G[h, :, pl.ds(pl.multiple_of(256 * xx, 256), 256)].astype(F32)
+        u = G[h, :, :, rows(xx, 256)].reshape(256, 256).astype(F32)
         scale = IG2[:, pl.ds(pl.multiple_of(512 * xx + 256 * h, 256), 256)]
         return jnp.sum(u * u * scale, axis=1, keepdims=True)
 
@@ -296,7 +311,7 @@
                 stage_two[0, e, d].wait_recv()
         sq = sq + squares(0, xx)
         cols = rows(xx, 256)
-        rhs = G[0, :, cols]
+        rhs = G[0, :, :, cols].reshape(256, 256)
 
         def add_chunk(s, carry, rhs=rhs, cols=cols, begin=(e == 0)):
             term = dot_nt(WV[s, 0, :, cols], rhs)
@@ -312,7 +327,7 @@
     inv = as_row(lax.rsqrt(sq * (1.0 / D) + EPS))
 
     def finish(s, top):
-        t = (ACC[s] + dot_nt(WV[s, 1], G[1])) * inv
+        t = (ACC[s] + dot_nt(WV[s, 1], G[1].reshape(256, 1024))) * inv
         ACC[s] = t
         return jnp.maximum(top, jnp.max(t, axis=0, keepdims=True))
 
@@ -330,10 +345,14 @@
 
     zero = jnp.zeros((1, 256), F32)
     total, pick = lax.fori_loop(0, 2, totals, (zero, zero))
-    st1[0] = jnp.concatenate([top, total, pick, jnp.zeros((5, 256), F32)], axis=0)
+    def split(v):
+        return [v[:, 0:128], v[:, 128:256]]
+
+    ST[k, x, y] = jnp.concatenate(split(top) + split(total) + split(pick) + [jnp.zeros((2, 128), F32)], axis=0)
     third = []
-    for d in NEAR_FIRST:
-        copy = remote(st1.at[0], st1.at[d], t1s.at[d], t1r.at[d], dev(x, k, ring(y, d)))
+    for i, (dx, dy, flip) in enumerate(everyone):
+        at = ST.at[k, x, y]
+        copy = remote(at, at, sts.at[i], str_.at[i], peers[i])
         copy.start()
         third.append(copy)
 
@@ -351,45 +370,35 @@
     nx.start()
     own_next = last_rows(0)
 
-    def combine(parts):
-        tops = [p[0:1] for p in parts]
-        m = functools.reduce(jnp.maximum, tops)
-        total = sum(p[1:2] * jnp.exp(t - m) for p, t in zip(parts, tops))
-        pick = sum(p[2:3] for p in parts)
-        return m, total, pick
-
+    nx.wait_recv()
     for copy in third:
-        copy.wait_recv()
-    m, total4, pick4 = combine([st1[d] for d in range(4)])
-    st2[me] = jnp.concatenate([m, total4, pick4, jnp.zeros((5, 256), F32)], axis=0)
-    fourth = []
-    for i, (d, flip) in enumerate(((0, 1), (1, 0), (1, 1), (3, 0), (3, 1), (2, 0), (2, 1))):
-        copy = remote(
-            st2.at[me], st2.at[me], t2s.at[i], t2r.at[i],
-            dev(ring(x, d), other if flip else k, y),
-        )
-        copy.start()
-        fourth.append(copy)
-    nx.wait_recv()
-    for copy in fourth:
         copy.wait_recv()
     lane1 = lax.broadcasted_iota(jnp.int32, (1, 64), 1)
     for plane in range(2):
-        m, total4, pick4 = combine([st2[2 * xx + plane] for xx in range(4)])
-        log_total = m + jnp.log(total4)
-        score = pick4 - log_total
+        parts = [ST[plane, xx, yy] for xx in range(4) for yy in range(4)]
+        tops = [p[0:2] for p in parts]
+        m = functools.reduce(jnp.maximum, tops)
+        whole = sum(p[2:4] * jnp.exp(t - m) for p, t in zip(parts, tops))
+        log_total = m + jnp.log(whole)
+        score = sum(p[4:6] for p in parts) - log_total
         for q in range(4):
             b = 2 * q + plane
-            at = slice(64 * q, 64 * q + 64)
+            at = 64 * (q % 2)
             live = (lane1 > 0) & (lane1 < counts[b])
-            out_node[pl.ds(b, 1), :] = jnp.where(live, score[:, at], 0.0)
+            out_node[pl.ds(b, 1), :] = jnp.where(live, score[q // 2 : q // 2 + 1, at : at + 64], 0.0)
             row = jnp.where(k == plane, own_next[q : q + 1], nx_recv[pl.ds(q, 1), :])
-            out_next[pl.ds(b, 1), :] = row - log_total[:, 64 * q : 64 * q + 1]
-
-    for copy in swaps + first + spread + list(second.values()) + list(stage_one.values()):
+            out_next[pl.ds(b, 1), :] = row - log_total[q // 2 : q // 2 + 1, at : at + 1]
+
+    for copy in swaps + list(wo_gathers.values()) + wo_forwards + first + spread[0] + spread[1]:
         copy.wait_send()
-    for copy in list(stage_two.values()) + third + fourth + [nx]:
+    for copy in list(stage_one.values()) + list(stage_two.values()) + third + [nx]:
         copy.wait_send()
+
+
+def emit(node, following, cache_rows, out_node, out_next, out_cache):
+    out_node[...] = node[...]
+    out_next[...] = following[...]
+    out_cache[...] = cache_rows[...]
 
 
 def shards(
@@ -403,20 +412,21 @@
     scalars = pl.BlockSpec(memory_space=pltpu.SMEM)
     vmem = pl.BlockSpec(memory_space=pltpu.VMEM)
     dma = pltpu.SemaphoreType.DMA
-    node, following, cache_rows = pl.pallas_call(
+    shapes = (
+        jax.ShapeDtypeStruct((8, NODES), F32),
+        jax.ShapeDtypeStruct((8, VW), F32),
+        jax.ShapeDtypeStruct((8, 128), BF16),
+    )
+    results = pl.pallas_call(
         body,
-        out_shape=(
-            jax.ShapeDtypeStruct((8, NODES), F32),
-            jax.ShapeDtypeStruct((8, VW), F32),
-            jax.ShapeDtypeStruct((8, 128), BF16),
-        ),
+        out_shape=shapes,
         in_specs=[anywhere] * 12 + [scalars] * 3,
         out_specs=(vmem, vmem, vmem),
         scratch_shapes=[
             pltpu.VMEM((256, D), BF16),
             pltpu.VMEM((1, D), F32),
             pltpu.VMEM((512, 640), BF16),
-            pltpu.VMEM((512, 512), BF16),
+            pltpu.VMEM((2, 1024, 512), BF16),
             pltpu.VMEM((1, D), F32),
             pltpu.VMEM((2, 2, VW, 1024), BF16),
             pltpu.VMEM((WIN, 128), BF16),
@@ -428,21 +438,19 @@
             pltpu.VMEM((256, 512), BF16),
             pltpu.VMEM((4, 64, 640), BF16),
             pltpu.VMEM((4, 64, 640), BF16),
-            pltpu.VMEM((2, 256, 256), BF16),
-            pltpu.VMEM((2, 256, 256), F32),
-            pltpu.VMEM((2, 4, 64, 256), BF16),
-            pltpu.VMEM((2, 4, 64, 256), BF16),
-            pltpu.VMEM((2, 256, 1024), BF16),
+            pltpu.VMEM((4, 64, 64), BF16),
+            pltpu.VMEM((2, 64, 256), BF16),
+            pltpu.VMEM((2, 4, 16, 1024), BF16),
+            pltpu.VMEM((2, 4, 64, 1024), BF16),
             pltpu.VMEM((2, VW, 256), F32),
             pltpu.VMEM((1, D), F32),
-            pltpu.VMEM((4, 8, 256), F32),
-            pltpu.VMEM((8, 8, 256), F32),
+            pltpu.VMEM((2, 4, 4, 8, 128), F32),
             pltpu.VMEM((8, VW), F32),
             pltpu.VMEM((8, VW), F32),
-            dma((24,)), dma((12,)), dma((12,)),
-            dma((4,)), dma((4,)), dma((2, 4)), dma((2, 4)), dma((2, 4)), dma((2, 4)),
+            dma((24,)), dma((12,)), dma((12,)), dma((2, 4)), dma((2, 4)), dma((2, 4)), dma((2, 4)),
+            dma((4,)), dma((4,)), dma((2, 4, 4)), dma((2, 4, 4)),
             dma((2, 4)), dma((2, 4)), dma((2, 4, 4)), dma((2, 4, 4)),
-            dma((4,)), dma((4,)), dma((8,)), dma((8,)), dma(()), dma(()),
+            dma((31,)), dma((31,)), dma(()), dma(()),
         ],
         compiler_params=pltpu.CompilerParams(
             collective_id=0, has_side_effects=True, vmem_limit_bytes=60 * 1024 * 1024
@@ -465,6 +473,9 @@
         lengths,
         accept_count,
     )
+    node, following, cache_rows = pl.pallas_call(
+        emit, out_shape=shapes, in_specs=[vmem] * 3, out_specs=(vmem,) * 3, name="emit"
+    )(*results)
     return node, following, cache_rows.reshape(1, 8, 1, 128)
 
 

time: 53.6 us -> 49.3 us (0.920)
  local copies, waits for them, and re-layouts: 3.88 us -> 0 us
    unnamed x3 -> x0, local copies, waits for them, and re-layouts: 3.88 us -> none
    pallas_call x1 -> x2, Pallas kernels: 48.8 us -> 48.5 us  [the longest x1 47.1 us: shards(): pl.pallas_call(body, out_shape=shapes, in_specs=[anywhere] * 12 + [scalar...]
where the time goes in v2:
time: 49.3 us; the launch traced here: 49.1 us
  Pallas kernels  48.5 us (98%)
  between operations  0.64 us (1%)
    pallas_call x1, Pallas kernels, shards(): pl.pallas_call(body, out_shape=shapes, in_specs=[anywhere] * 12 + [scalar...  47.1 us
    pallas_call x1, Pallas kernels, shards(): pl.pallas_call(emit, out_shape=shapes, in_specs=[vmem] * 3, out_specs=(vm...  1.38 us

profile of v2, /device:TPU:1, one launch (start us, length us, event | category | flops | bytes accessed | tf_op | source)
XLA Modules:
  0.0 49.1 jit_solution(791586728234537358)
XLA Ops:
  0.6 47.1 %verify.1 = (f32[8,64]{1,0:T(8,128)}, f32[8,1002]{1,0:T(8,128)}, bf16[8,128]{1,0:T(8,128)(2,1)}) custom-call(bf16[512,2048]{1,0:T(8,128)(2,1)} %hid.1, f32[1,2048]{1,0:T(1,128)} %bitcast.9, bf16[256,512]{1,0:T(8,128)(2,1)} %wq.1, bf16[256,128]{1,0:T(8,128)(2,1)} %bitcast.8, bf16[512,256]{1,0:T(8,128)(2,1)} %wo.1, f32[1,2048]{1,0:T(1,128)} %bitcast.10, ...), custom_call_target="tpu_custom_call" | custom-call | tf_op jit(solution)/shard_map/verify/pallas_call | solution.py:420
  47.7 1.4 %emit.1 = (f32[8,64]{1,0:T(8,128)}, f32[8,1002]{1,0:T(8,128)}, bf16[8,128]{1,0:T(8,128)(2,1)}) custom-call(f32[8,64]{1,0:T(8,128)} %get-tuple-element.9.node, f32[8,1002]{1,0:T(8,128)} %get-tuple-element.10.following, bf16[8,128]{1,0:T(8,128)(2,1)} %get-tuple-element.11.cache_rows), custom_call_target="tpu_custom_call" | custom-call | tf_op jit(solution)/shard_map/emit/pallas_call | solution.py:476
